TPU v7x, 256 devices: a whole 4x4x8 slice. The times are simulated.
256 devices in a mesh: expert: 64 (over y, z, core), dp: 4 (over x).
Axes of the slice: x: 4, y: 4, z: 8, core: 2. Of those that a mesh axis runs over, the one named last changes fastest.
Arguments:
- grad_rows: bfloat16 [4, 32768, 2048], P('dp', 'expert'), may hold values from -6 to 6
- counts: int32 [4, 64, 64], P('dp', 'expert'), may hold values from 0 to 10, as said below
- order: int32 [4, 32768], P('dp', 'expert'), may hold values from 0 to 511, as said below
- hidden: bfloat16 [4, 64, 640, 768], P('dp', 'expert'), may hold values from -0.29882812 to 0.29882812
- down_weight: bfloat16 [64, 768, 2048], P('expert'), may hold values from -0.21875 to 0.21875
- error_in: bfloat16 [4, 64, 768, 2048], P('dp', 'expert'), may hold values from -6 to 6
- q_init: bfloat16 [64, 2048, 64], P('expert'), may hold values from -6 to 6
Outputs:
- input_grad: bfloat16 [4, 32768, 768], P('dp', 'expert')
- p_basis: float32 [64, 768, 64], P('expert')
- q_factor: float32 [64, 2048, 64], P('expert')
- error_out: bfloat16 [4, 64, 768, 2048], P('dp', 'expert')
Inputs may be any that keep to these rules, and one draw needn't show every extreme that they name: On each device (r, s) the 64 counts sum to 512; in every draw one expert receives exactly 10 rows from every device. `order`: each device's 512 entries are a permutation of 0 to 511.
All inputs are finite; a program needn't handle non-finite values.
Results may differ from a plain program's by a relative error of at most 0.001.
Values may be sent and summed in bfloat16 or wider, within the bound.
A program may use at most 128 MiB of HBM per device.

v0:
```python
import jax
import jax.numpy as jnp
from jax import lax
from jax.sharding import PartitionSpec as P


def orthonormal_rows(p_rows, gram):
    lower = jnp.linalg.cholesky(gram)
    return lax.linalg.triangular_solve(lower, p_rows, left_side=False, lower=True, transpose_a=True)


def shards(grad_rows, counts, order, hidden, down_weight, error_in, q_init):
    local_rows = grad_rows[0]
    route_count = counts[0, 0]
    order_local = order[0]
    experts = route_count.shape[0]
    total_rows = local_rows.shape[0]
    width = local_rows.shape[1]
    saved_hidden = hidden[0, 0]
    hidden_units = saved_hidden.shape[1]
    capacity = saved_hidden.shape[0] // experts
    expert_weight = down_weight[0]
    route_ends = jnp.cumsum(route_count)
    route_starts = route_ends - route_count
    slot_ids = jnp.arange(capacity, dtype=jnp.int32)
    pick_index = jnp.minimum(route_starts[:, None] + slot_ids[None, :], total_rows - 1)
    slot_valid = slot_ids[None, :] < route_count[:, None]
    outgoing = local_rows[pick_index.reshape(-1)].reshape(experts, capacity, width)
    outgoing = jnp.where(slot_valid[:, :, None], outgoing, jnp.zeros((), jnp.bfloat16))
    arrived = lax.all_to_all(outgoing, "expert", split_axis=0, concat_axis=0, tiled=True)
    returned = lax.all_to_all(
        jnp.einsum(
            "ncd,fd->ncf", arrived, expert_weight, preferred_element_type=jnp.float32
        ).astype(jnp.bfloat16),
        "expert",
        split_axis=0,
        concat_axis=0,
        tiled=True,
    )
    arrived_flat = arrived.reshape(experts * capacity, width)
    grad_w = lax.dot_general(
        saved_hidden, arrived_flat, (((0,), (0,)), ((), ())), preferred_element_type=jnp.float32
    )
    moment = grad_w + error_in[0, 0].astype(jnp.float32)
    q_start = q_init[0].astype(jnp.float32)
    partial_p = jnp.dot(moment, q_start, precision=lax.Precision.HIGHEST)
    p_total = lax.psum(partial_p, "dp")
    p_basis = orthonormal_rows(
        p_total, jnp.dot(p_total.T, p_total, precision=lax.Precision.HIGHEST)
    )
    partial_q = lax.dot_general(
        moment, p_basis, (((0,), (0,)), ((), ())), precision=lax.Precision.HIGHEST
    )
    replicas = lax.axis_size("dp")
    q_factor = lax.psum(partial_q, "dp") / replicas
    approximation = jnp.dot(p_basis, q_factor.T, precision=lax.Precision.HIGHEST)
    error_new = (moment - approximation).astype(jnp.bfloat16)
    returned_flat = returned.reshape(experts * capacity, hidden_units)
    expert_of = jnp.sum((route_ends[None, :] <= order_local[:, None]).astype(jnp.int32), axis=1)
    expert_ids = jnp.arange(experts, dtype=jnp.int32)
    onehot = (expert_of[:, None] == expert_ids[None, :]).astype(jnp.int32)
    row_base = jnp.sum(onehot * (expert_ids * capacity - route_starts)[None, :], axis=1)
    position = row_base + order_local
    input_grad = returned_flat[position]
    return (input_grad[None], p_basis[None], q_factor[None], error_new[None, None])


def solution(mesh):
    placed = (
        P("dp", "expert", None),
        P("dp", "expert", None),
        P("dp", "expert"),
        P("dp", "expert", None, None),
        P("expert", None, None),
        P("dp", "expert", None, None),
        P("expert", None, None),
    )
    return jax.shard_map(
        shards,
        mesh=mesh,
        in_specs=placed,
        out_specs=(
            P("dp", "expert", None),
            P("expert", None, None),
            P("expert", None, None),
            P("dp", "expert", None, None),
        ),
        check_vma=False,
    )
```

profile of v0, /device:TPU:8, one launch (start us, length us, event | category | flops | bytes accessed | tf_op | source)
XLA Modules:
  0.0 299.9 jit_solution(14025516916071478414)
XLA Ops:
  7.2 0.0 copy-start
  7.2 0.9 iota_compare_fusion.3
  8.1 0.8 copy.31
  8.9 0.1 reduce-window.7
  9.0 0.1 reduce.6
  9.1 0.7 multiply_subtract_fusion
  9.8 0.1 add_minimum_fusion
  9.8 0.1 min.19
  10.0 8.8 %gather_fusion = bf16[640,2048]{1,0:T(8,128)(2,1)} fusion(bf16[512,2048]{1,0:T(8,128)(2,1)} %bitcast.52, s32[1024]{0:T(1024)S(1)} %pad_clamp_fusion.1), kind=kCustom, calls=%fused_computation | custom fusion | bytes 5245440 | tf_op jit(solution)/shard_map/gather | solution.py:28
  18.8 5.4 %reshape.154 = bf16[64,10,2048]{2,1,0:T(8,128)(2,1)} reshape(bf16[640,2048]{1,0:T(8,128)(2,1)} %gather_fusion) | data formatting | bytes 5242880 | tf_op jit(solution)/shard_map/reshape | solution.py:28
  24.2 4.5 %broadcast_select_fusion = bf16[64,10,2048]{2,1,0:T(8,128)(2,1)} fusion(bf16[64,10,2048]{2,1,0:T(8,128)(2,1)} %reshape.154, pred[64,10]{1,0:T(8,128)(4,1)S(1)} %iota_compare_fusion.3), kind=kLoop, calls=%fused_computation.4 | loop fusion | flops 1310720 | bytes 5243520 | tf_op jit(solution)/shard_map/jit(_where)/select_n | solution.py:29
  28.6 12.3 %all-to-all-start = ((bf16[64,10,2048]{2,1,0:T(8,128)(2,1)}), bf16[64,10,2048]{2,1,0:T(8,128)(2,1)}, u32[]{:S(2)}, u32[]{:S(2)}) async-start(bf16[64,10,2048]{2,1,0:T(8,128)(2,1)} %broadcast_select_fusion), calls=%async_computation | async-start | bytes 8388608 | tf_op jit(solution)/shard_map/all_to_all | solution.py:30
  40.9 0.2 all-reduce.3.cloned.1.call-start
  41.2 4.6 %copy.34 = bf16[1,1,768,2048]{2,3,1,0:T(8,128)(2,1)} copy(bf16[1,1,768,2048]{3,2,1,0:T(8,128)(2,1)} %param.12) | data formatting | bytes 6291456 | tf_op args[5]
  45.8 90.0 %all-to-all-done = bf16[64,10,2048]{2,1,0:T(8,128)(2,1)} async-done(((bf16[64,10,2048]{2,1,0:T(8,128)(2,1)}), bf16[64,10,2048]{2,1,0:T(8,128)(2,1)}, u32[]{:S(2)}, u32[]{:S(2)}) %all-to-all-start) | async-done | bytes 2621472 | tf_op jit(solution)/shard_map/all_to_all | solution.py:30
  135.8 5.5 %reshape.156 = bf16[640,2048]{1,0:T(8,128)(2,1)} reshape(bf16[64,10,2048]{2,1,0:T(8,128)(2,1)} %all-to-all-done) | data formatting | bytes 5242880 | tf_op jit(solution)/shard_map/reshape | solution.py:40
  141.3 0.0 copy-start.3
  141.3 5.8 %convert_add_fusion = f32[768,2048]{0,1:T(8,128)S(1)} fusion(bf16[640,2048]{1,0:T(8,128)(2,1)} %reshape.156, bf16[1,1,768,2048]{2,3,1,0:T(8,128)(2,1)} %copy.34, bf16[1,1,640,768]{3,2,1,0:T(8,128)(2,1)} %param.10), kind=kOutput, calls=%fused_computation.2 | convolution fusion | flops 2016411648 | bytes 13041664 | tf_op jit(solution)/shard_map/dot_general | solution.py:41
  147.1 0.0 copy-start.1
  147.1 2.7 copy-done.1
  149.8 0.0 copy-done.3
  149.8 3.2 %fusion.11 = f32[768,64]{0,1:T(8,128)} fusion(f32[768,2048]{0,1:T(8,128)S(1)} %convert_add_fusion, bf16[1,2048,64]{1,2,0:T(8,128)(2,1)S(1)} %copy-done.3), kind=kOutput, calls=%fused_computation.13 | convolution fusion | flops 1207959552 | bytes 6750208 | tf_op jit(solution)/shard_map/dot_general | solution.py:46
  153.0 0.0 all-reduce.3.cloned.1.call-update
  153.0 0.0 copy-done
  153.0 7.0 %fusion.4 = bf16[64,10,768]{2,0,1:T(8,128)(2,1)S(1)} fusion(bf16[1,768,2048]{2,1,0:T(8,128)(2,1)S(1)} %copy-done, bf16[64,10,2048]{2,1,0:T(8,128)(2,1)} %all-to-all-done), kind=kOutput, calls=%fused_computation.9 | convolution fusion | flops 2013757440 | bytes 6750208 | tf_op jit(solution)/shard_map/ncd,fd->ncf/dot_general | solution.py:32
  159.9 1.7 copy.33
  161.6 6.9 %all-to-all-start.1 = ((bf16[64,10,768]{2,1,0:T(8,128)(2,1)}), bf16[64,10,768]{2,1,0:T(8,128)(2,1)}, u32[]{:S(2)}, u32[]{:S(2)}) async-start(bf16[64,10,768]{2,1,0:T(8,128)(2,1)} %copy.33), calls=%async_computation.1 | async-start | bytes 3145728 | tf_op jit(solution)/shard_map/all_to_all | solution.py:31
  168.6 0.3 all-reduce.5.cloned.1.call-start
  168.9 28.4 %all-reduce.3.cloned.1.call-done = f32[768,64]{0,1:T(8,128)} async-done(((f32[768,64]{0,1:T(8,128)}), f32[768,64]{0,1:T(8,128)}) %all-reduce.3.cloned.1.call-update) | async-done | bytes 196624 | tf_op jit(solution)/shard_map/psum | solution.py:47
  197.3 1.3 fusion.20
  198.6 0.1 copy.35
  198.7 5.8 %cholesky.16 = f32[64,64]{1,0:T(8,128)S(1)} custom-call(f32[64,64]{1,0:T(8,128)S(1)} %fusion.17), custom_call_target="Cholesky" | custom-call | tf_op jit(solution)/shard_map/jit(cholesky)/cholesky | solution.py:8
  204.6 0.6 compare_reduce_fusion
  205.2 0.7 fusion.14
  205.9 4.9 %custom-call.6 = f32[1,64,64]{1,2,0:T(8,128)S(1)} custom-call(f32[1,64,64]{2,1,0:T(8,128)S(1)} %fusion.14), custom_call_target="InvertDiagBlocksLowerTriangular" | custom-call | tf_op jit(solution)/shard_map/triangular_solve | solution.py:9
  210.8 1.3 fusion.15
  212.1 0.0 copy-start.2
  212.1 0.0 copy-start.4
  212.1 9.8 %fusion.21 = f32[2048,64]{0,1:T(8,128)} fusion(f32[768,2048]{0,1:T(8,128)} %copy-done.1, f32[768,64]{0,1:T(8,128)S(1)} %fusion.15), kind=kOutput, calls=%fused_computation.41 | convolution fusion | flops 1207959552 | bytes 7012352 | tf_op jit(solution)/shard_map/dot_general | solution.py:51
  221.9 0.0 all-reduce.5.cloned.1.call-update
  221.9 0.0 copy-done.4
  222.0 0.1 convert_reduce_fusion
  222.1 0.1 select_reduce_fusion
  222.2 48.5 %all-reduce.5.cloned.1.call-done = f32[2048,64]{0,1:T(8,128)} async-done(((f32[2048,64]{0,1:T(8,128)}), f32[2048,64]{0,1:T(8,128)}) %all-reduce.5.cloned.1.call-update) | async-done | bytes 524304 | tf_op jit(solution)/shard_map/psum | solution.py:55
  270.7 0.0 copy-done.2
  270.7 8.5 %fusion.2 = bf16[1,1,768,2048]{2,3,1,0:T(8,128)(2,1)} fusion(f32[768,2048]{0,1:T(8,128)} %copy-done.1, f32[768,64]{0,1:T(8,128)S(1)} %fusion.15, f32[2048,64]{0,1:T(8,128)} %all-reduce.5.cloned.1.call-done), kind=kOutput, calls=%fused_computation.7 | convolution fusion | flops 1211236352 | bytes 10158080 | tf_op jit(solution)/shard_map/dot_general | solution.py:56
  279.1 4.6 %copy.37 = bf16[1,1,768,2048]{3,2,1,0:T(8,128)(2,1)} copy(bf16[1,1,768,2048]{2,3,1,0:T(8,128)(2,1)} %fusion.2) | data formatting | bytes 6291456
  283.8 1.9 multiply_bitcast_fusion
  285.6 0.0 all-to-all-done.1
  285.6 3.0 %reshape.155 = bf16[640,768]{1,0:T(8,128)(2,1)} reshape(bf16[64,10,768]{2,1,0:T(8,128)(2,1)} %all-to-all-done.1) | data formatting | bytes 1966080 | tf_op jit(solution)/shard_map/reshape | solution.py:58
  288.7 4.4 %gather_fusion.1 = bf16[512,768]{1,0:T(8,128)(2,1)} fusion(bf16[640,768]{1,0:T(8,128)(2,1)} %reshape.155, s32[1024]{0:T(1024)S(1)} %pad_clamp_fusion), kind=kCustom, calls=%fused_computation.1 | custom fusion | bytes 1574912 | tf_op jit(solution)/shard_map/gather | solution.py:64
  (6 shorter events, 0.1 us)
Async XLA Ops:
  7.2 145.8 %copy-start = (bf16[1,768,2048]{2,1,0:T(8,128)(2,1)S(1)}, bf16[1,768,2048]{2,1,0:T(8,128)(2,1)}, u32[]{:S(2)}) copy-start(bf16[1,768,2048]{2,1,0:T(8,128)(2,1)} %param.11) | copy-start | bytes 9437188
  28.6 107.2 %all-to-all-start = ((bf16[64,10,2048]{2,1,0:T(8,128)(2,1)}), bf16[64,10,2048]{2,1,0:T(8,128)(2,1)}, u32[]{:S(2)}, u32[]{:S(2)}) async-start(bf16[64,10,2048]{2,1,0:T(8,128)(2,1)} %broadcast_select_fusion), calls=%async_computation | async-start | bytes 8388608 | tf_op jit(solution)/shard_map/all_to_all | solution.py:30
  40.9 156.3 %all-reduce.3.cloned.1.call-start = ((), (), s32[]{:S(2)}) async-start(), calls=%async_computation.2 | async-start | bytes 393216 | tf_op jit(solution)/shard_map/psum | solution.py:47
  141.3 8.5 %copy-start.3 = (bf16[1,2048,64]{1,2,0:T(8,128)(2,1)S(1)}, bf16[1,2048,64]{1,2,0:T(8,128)(2,1)}, u32[]{:S(2)}) copy-start(bf16[1,2048,64]{1,2,0:T(8,128)(2,1)} %param.13) | copy-start | bytes 786436
  147.1 2.7 copy-start.1
  161.6 124.0 %all-to-all-start.1 = ((bf16[64,10,768]{2,1,0:T(8,128)(2,1)}), bf16[64,10,768]{2,1,0:T(8,128)(2,1)}, u32[]{:S(2)}, u32[]{:S(2)}) async-start(bf16[64,10,768]{2,1,0:T(8,128)(2,1)} %copy.33), calls=%async_computation.1 | async-start | bytes 3145728 | tf_op jit(solution)/shard_map/all_to_all | solution.py:31
  168.6 102.1 %all-reduce.5.cloned.1.call-start = ((), (), s32[]{:S(2)}) async-start(), calls=%async_computation.3 | async-start | bytes 1048576 | tf_op jit(solution)/shard_map/psum | solution.py:55
  212.1 58.6 %copy-start.2 = (f32[768,64]{0,1:T(8,128)}, f32[768,64]{0,1:T(8,128)S(1)}, u32[]{:S(2)}) copy-start(f32[768,64]{0,1:T(8,128)S(1)} %fusion.15) | copy-start | bytes 589828
  212.1 9.9 %copy-start.4 = (s32[1,512]{1,0:T(1,128)S(1)}, s32[1,512]{1,0:T(1,128)}, u32[]{:S(2)}) copy-start(s32[1,512]{1,0:T(1,128)} %param.9) | copy-start | bytes 6148
Sparse Core Ops, SparseCore 0:
  153.1 44.1 all-reduce.2
  222.1 48.5 all-reduce.4
where the time goes:
time: 301 us; the launch traced here: 300 us
  waiting for transfers between devices  167 us (55%)
  local copies, waits for them, and re-layouts  41.8 us (14%)
  matrix products  36.8 us (12%)
  other arithmetic  20.5 us (7%)
  starting transfers between devices  19.7 us (7%)
  between operations  14.2 us (5%)
    all_to_all x1, waiting for transfers between devices, shards(): lax.all_to_all(outgoing, 'expert', split_axis=0, concat_axis=0, tiled=True)  90 us
    psum x1, waiting for transfers between devices, shards(): q_factor = lax.psum(partial_q, 'dp') / replicas  48.5 us
    psum x1, waiting for transfers between devices, shards(): p_total = lax.psum(partial_p, 'dp')  28.4 us
    all_to_all x1, starting transfers between devices, shards(): lax.all_to_all(outgoing, 'expert', split_axis=0, concat_axis=0, tiled=True)  12.3 us
    unnamed x12, local copies, waits for them, and re-layouts  11.9 us
    dot_general x1, matrix products, shards(): lax.dot_general(moment, p_basis, (((0,), (0,)), ((), ())), precision=lax....  9.82 us
    gather x1, local copies, waits for them, and re-layouts, shards(): local_rows[pick_index.reshape(-1)].reshape(experts, capacity, width)  8.78 us
    dot_general x1, matrix products, shards(): jnp.dot(p_basis, q_factor.T, precision=lax.Precision.HIGHEST)  8.46 us
  transfers between devices with their start and end apart: 4, of which 3 were waited for; matrix products, arithmetic and copies ran while one was open for 18% of the time, Pallas kernels for 0%

commit v1 on v0

--- a/solution.py
+++ b/solution.py
@@ -52,7 +52,7 @@
         moment, p_basis, (((0,), (0,)), ((), ())), precision=lax.Precision.HIGHEST
     )
     replicas = lax.axis_size("dp")
-    q_factor = lax.psum(partial_q, "dp") / replicas
+    q_factor = jnp.sum(lax.all_gather(partial_q, "dp"), axis=0) / replicas
     approximation = jnp.dot(p_basis, q_factor.T, precision=lax.Precision.HIGHEST)
     error_new = (moment - approximation).astype(jnp.bfloat16)
     returned_flat = returned.reshape(experts * capacity, hidden_units)

time: 301 us -> 319 us (1.060)
  waiting for transfers between devices: 167 us -> 173 us
  local copies, waits for them, and re-layouts: 41.8 us -> 45.4 us
  starting transfers between devices: 19.7 us -> 23.3 us
    psum x1 -> x0, waiting for transfers between devices: 48.5 us -> none  [shards(): q_factor = lax.psum(partial_q, 'dp') / replicas]
    all_to_all x1, waiting for transfers between devices: 0.01 us -> 38.3 us  [shards(): lax.all_to_all(jnp.einsum('ncd,fd->ncf', arrived, expert_weight, preferre...]
    psum x1, waiting for transfers between devices: 28.4 us -> 44 us  [shards(): p_total = lax.psum(partial_p, 'dp')]
    all_to_all x1, starting transfers between devices: 6.94 us -> 10.7 us  [shards(): lax.all_to_all(jnp.einsum('ncd,fd->ncf', arrived, expert_weight, preferre...]
    reduce_sum x0 -> x1, other arithmetic: none -> 3.7 us  [shards(): q_factor = jnp.sum(lax.all_gather(partial_q, 'dp'), axis=0) / replicas]
    all_gather x0 -> x1, local copies, waits for them, and re-layouts: none -> 3.62 us  [shards(): q_factor = jnp.sum(lax.all_gather(partial_q, 'dp'), axis=0) / replicas]
    unnamed x12 -> x14, local copies, waits for them, and re-layouts: 11.9 us -> 11.9 us
  transfers between devices with their start and end apart: 4 -> 4, of which waited for: 3 -> 3; matrix products, arithmetic and copies ran while one was open for 18% -> 7% of each run, Pallas kernels for 0% -> 0%
where the time goes in v1:
time: 319 us; the launch traced here: 316 us
  waiting for transfers between devices  173 us (54%)
  local copies, waits for them, and re-layouts  45.4 us (14%)
  matrix products  37.3 us (12%)
  starting transfers between devices  23.3 us (7%)
  other arithmetic  23.1 us (7%)
  between operations  14.2 us (4%)
    all_to_all x1, waiting for transfers between devices, shards(): lax.all_to_all(outgoing, 'expert', split_axis=0, concat_axis=0, tiled=True)  90.2 us
    psum x1, waiting for transfers between devices, shards(): p_total = lax.psum(partial_p, 'dp')  44 us
    all_to_all x1, waiting for transfers between devices, shards(): lax.all_to_all(jnp.einsum('ncd,fd->ncf', arrived, expert_weight, preferre...  38.3 us
    all_to_all x1, starting transfers between devices, shards(): lax.all_to_all(outgoing, 'expert', split_axis=0, concat_axis=0, tiled=True)  12.3 us
    unnamed x14, local copies, waits for them, and re-layouts  11.9 us
    all_to_all x1, starting transfers between devices, shards(): lax.all_to_all(jnp.einsum('ncd,fd->ncf', arrived, expert_weight, preferre...  10.7 us
    dot_general x1, matrix products, shards(): lax.dot_general(moment, p_basis, (((0,), (0,)), ((), ())), precision=lax....  9.81 us
    dot_general x1, matrix products, shards(): jnp.dot(p_basis, q_factor.T, precision=lax.Precision.HIGHEST)  8.94 us
  transfers between devices with their start and end apart: 4, of which 3 were waited for; matrix products, arithmetic and copies ran while one was open for 7% of the time, Pallas kernels for 0%

profile of v1, /device:TPU:8, one launch (start us, length us, event | category | flops | bytes accessed | tf_op | source)
XLA Modules:
  0.0 315.9 jit_solution(3867108169862434019)
XLA Ops:
  7.2 0.0 copy-start
  7.2 0.9 iota_compare_fusion.3
  8.1 0.8 copy.31
  8.9 0.1 reduce-window.7
  9.0 0.1 reduce.6
  9.1 0.7 multiply_subtract_fusion
  9.8 0.1 add_minimum_fusion
  9.8 0.1 min.19
  10.0 8.8 %gather_fusion = bf16[640,2048]{1,0:T(8,128)(2,1)} fusion(bf16[512,2048]{1,0:T(8,128)(2,1)} %bitcast.54, s32[1024]{0:T(1024)S(1)} %pad_clamp_fusion.1), kind=kCustom, calls=%fused_computation | custom fusion | bytes 5245440 | tf_op jit(solution)/shard_map/gather | solution.py:28
  18.8 5.4 %reshape.163 = bf16[64,10,2048]{2,1,0:T(8,128)(2,1)} reshape(bf16[640,2048]{1,0:T(8,128)(2,1)} %gather_fusion) | data formatting | bytes 5242880 | tf_op jit(solution)/shard_map/reshape | solution.py:28
  24.2 4.5 %broadcast_select_fusion = bf16[64,10,2048]{2,1,0:T(8,128)(2,1)} fusion(bf16[64,10,2048]{2,1,0:T(8,128)(2,1)} %reshape.163, pred[64,10]{1,0:T(8,128)(4,1)S(1)} %iota_compare_fusion.3), kind=kLoop, calls=%fused_computation.4 | loop fusion | flops 1310720 | bytes 5243520 | tf_op jit(solution)/shard_map/jit(_where)/select_n | solution.py:29
  28.6 12.3 %all-to-all-start = ((bf16[64,10,2048]{2,1,0:T(8,128)(2,1)}), bf16[64,10,2048]{2,1,0:T(8,128)(2,1)}, u32[]{:S(2)}, u32[]{:S(2)}) async-start(bf16[64,10,2048]{2,1,0:T(8,128)(2,1)} %broadcast_select_fusion), calls=%async_computation | async-start | bytes 8388608 | tf_op jit(solution)/shard_map/all_to_all | solution.py:30
  40.9 0.0 all-reduce.2.cloned.1.call-start
  41.0 4.6 %copy.34 = bf16[1,1,768,2048]{2,3,1,0:T(8,128)(2,1)} copy(bf16[1,1,768,2048]{3,2,1,0:T(8,128)(2,1)} %param.12) | data formatting | bytes 6291456 | tf_op args[5]
  45.6 90.2 %all-to-all-done = bf16[64,10,2048]{2,1,0:T(8,128)(2,1)} async-done(((bf16[64,10,2048]{2,1,0:T(8,128)(2,1)}), bf16[64,10,2048]{2,1,0:T(8,128)(2,1)}, u32[]{:S(2)}, u32[]{:S(2)}) %all-to-all-start) | async-done | bytes 2621472 | tf_op jit(solution)/shard_map/all_to_all | solution.py:30
  135.8 5.5 %reshape.165 = bf16[640,2048]{1,0:T(8,128)(2,1)} reshape(bf16[64,10,2048]{2,1,0:T(8,128)(2,1)} %all-to-all-done) | data formatting | bytes 5242880 | tf_op jit(solution)/shard_map/reshape | solution.py:40
  141.3 0.0 copy-start.4
  141.3 5.8 %convert_add_fusion = f32[768,2048]{0,1:T(8,128)S(1)} fusion(bf16[640,2048]{1,0:T(8,128)(2,1)} %reshape.165, bf16[1,1,768,2048]{2,3,1,0:T(8,128)(2,1)} %copy.34, bf16[1,1,640,768]{3,2,1,0:T(8,128)(2,1)} %param.10), kind=kOutput, calls=%fused_computation.2 | convolution fusion | flops 2016411648 | bytes 13041664 | tf_op jit(solution)/shard_map/dot_general | solution.py:41
  147.1 0.0 copy-start.1
  147.1 2.7 copy-done.1
  149.8 0.0 copy-done.4
  149.8 3.2 fusion.11
  153.0 0.0 all-reduce.2.cloned.1.call-update
  153.0 0.2 all-gather.3.cloned.1.call-start
  153.2 44.0 %all-reduce.2.cloned.1.call-done = f32[768,64]{0,1:T(8,128)} async-done(((f32[768,64]{0,1:T(8,128)}), f32[768,64]{0,1:T(8,128)}) %all-reduce.2.cloned.1.call-update) | async-done | bytes 196624 | tf_op jit(solution)/shard_map/psum | solution.py:47
  197.3 1.3 fusion.20
  198.6 0.1 copy.35
  198.7 5.8 %cholesky.16 = f32[64,64]{1,0:T(8,128)S(1)} custom-call(f32[64,64]{1,0:T(8,128)S(1)} %fusion.17), custom_call_target="Cholesky" | custom-call | tf_op jit(solution)/shard_map/jit(cholesky)/cholesky | solution.py:8
  204.6 0.6 compare_reduce_fusion
  205.2 0.7 fusion.14
  205.9 4.9 %custom-call.6 = f32[1,64,64]{1,2,0:T(8,128)S(1)} custom-call(f32[1,64,64]{2,1,0:T(8,128)S(1)} %fusion.14), custom_call_target="InvertDiagBlocksLowerTriangular" | custom-call | tf_op jit(solution)/shard_map/triangular_solve | solution.py:9
  210.8 1.3 fusion.15
  212.1 0.0 copy-start.3
  212.1 9.8 %fusion.21 = f32[2048,64]{0,1:T(8,128)} fusion(f32[768,2048]{0,1:T(8,128)} %copy-done.1, f32[768,64]{0,1:T(8,128)S(1)} %fusion.15), kind=kOutput, calls=%fused_computation.41 | convolution fusion | flops 1207959552 | bytes 7012352 | tf_op jit(solution)/shard_map/dot_general | solution.py:51
  221.9 0.0 all-gather.3.cloned.1.call-update
  221.9 0.0 copy-done
  221.9 7.0 %fusion.4 = bf16[64,10,768]{2,0,1:T(8,128)(2,1)S(1)} fusion(bf16[1,768,2048]{2,1,0:T(8,128)(2,1)S(1)} %copy-done, bf16[64,10,2048]{2,1,0:T(8,128)(2,1)} %all-to-all-done), kind=kOutput, calls=%fused_computation.9 | convolution fusion | flops 2013757440 | bytes 6750208 | tf_op jit(solution)/shard_map/ncd,fd->ncf/dot_general | solution.py:32
  228.9 0.0 copy-start.5
  228.9 1.7 copy.33
  230.6 10.7 %all-to-all-start.1 = ((bf16[64,10,768]{2,1,0:T(8,128)(2,1)}), bf16[64,10,768]{2,1,0:T(8,128)(2,1)}, u32[]{:S(2)}, u32[]{:S(2)}) async-start(bf16[64,10,768]{2,1,0:T(8,128)(2,1)} %copy.33), calls=%async_computation.1 | async-start | bytes 3145728 | tf_op jit(solution)/shard_map/all_to_all | solution.py:31
  241.4 0.0 copy-done.5
  241.4 0.1 convert_reduce_fusion
  241.5 0.1 select_reduce_fusion
  241.6 38.3 %all-to-all-done.1 = bf16[64,10,768]{2,1,0:T(8,128)(2,1)} async-done(((bf16[64,10,768]{2,1,0:T(8,128)(2,1)}), bf16[64,10,768]{2,1,0:T(8,128)(2,1)}, u32[]{:S(2)}, u32[]{:S(2)}) %all-to-all-start.1) | async-done | bytes 983072 | tf_op jit(solution)/shard_map/all_to_all | solution.py:31
  279.9 3.0 reshape.164
  282.9 4.4 %gather_fusion.1 = bf16[512,768]{1,0:T(8,128)(2,1)} fusion(bf16[640,768]{1,0:T(8,128)(2,1)} %reshape.164, s32[1024]{0:T(1024)S(1)} %pad_clamp_fusion), kind=kCustom, calls=%fused_computation.1 | custom fusion | bytes 1574912 | tf_op jit(solution)/shard_map/gather | solution.py:64
  287.3 0.0 all-gather.3.cloned.1.call-done
  287.3 3.6 %reshape.183 = f32[4,2048,64]{1,0,2:T(4,128)} reshape(f32[8192,64]{0,1:T(8,128)} %all-gather.3.cloned.1.call-done) | data formatting | bytes 4194304 | tf_op jit(solution)/shard_map/all_gather | solution.py:55
  291.0 3.7 %reduce_sum.32 = f32[2048,64]{0,1:T(8,128)} reduce(f32[4,2048,64]{1,0,2:T(4,128)} %reshape.183, f32[]{:T(128)} %constant.59.clone.1), dimensions={0}, to_apply=%region_6.7 | reduce | flops 393216 | bytes 2621444 | tf_op jit(solution)/shard_map/reduce_sum | solution.py:55
  294.7 0.0 copy-done.3
  294.7 0.0 copy-start.2
  294.7 8.9 %fusion.2 = bf16[1,1,768,2048]{2,3,1,0:T(8,128)(2,1)} fusion(f32[768,2048]{0,1:T(8,128)} %copy-done.1, f32[768,64]{0,1:T(8,128)S(1)} %fusion.15, f32[2048,64]{0,1:T(8,128)} %reduce_sum.32), kind=kOutput, calls=%fused_computation.7 | convolution fusion | flops 1211236352 | bytes 10158080 | tf_op jit(solution)/shard_map/dot_general | solution.py:56
  303.6 0.0 copy-done.2
  303.6 0.8 multiply_bitcast_fusion
  304.5 4.6 %copy.37 = bf16[1,1,768,2048]{3,2,1,0:T(8,128)(2,1)} copy(bf16[1,1,768,2048]{2,3,1,0:T(8,128)(2,1)} %fusion.2) | data formatting | bytes 6291456
  (6 shorter events, 0.1 us)
Async XLA Ops:
  7.2 214.8 %copy-start = (bf16[1,768,2048]{2,1,0:T(8,128)(2,1)S(1)}, bf16[1,768,2048]{2,1,0:T(8,128)(2,1)}, u32[]{:S(2)}) copy-start(bf16[1,768,2048]{2,1,0:T(8,128)(2,1)} %param.11) | copy-start | bytes 9437188
  28.6 107.2 %all-to-all-start = ((bf16[64,10,2048]{2,1,0:T(8,128)(2,1)}), bf16[64,10,2048]{2,1,0:T(8,128)(2,1)}, u32[]{:S(2)}, u32[]{:S(2)}) async-start(bf16[64,10,2048]{2,1,0:T(8,128)(2,1)} %broadcast_select_fusion), calls=%async_computation | async-start | bytes 8388608 | tf_op jit(solution)/shard_map/all_to_all | solution.py:30
  40.9 156.3 %all-reduce.2.cloned.1.call-start = ((), (), s32[]{:S(2)}) async-start(), calls=%async_computation.2 | async-start | bytes 393216 | tf_op jit(solution)/shard_map/psum | solution.py:47
  141.3 8.5 %copy-start.4 = (bf16[1,2048,64]{1,2,0:T(8,128)(2,1)S(1)}, bf16[1,2048,64]{1,2,0:T(8,128)(2,1)}, u32[]{:S(2)}) copy-start(bf16[1,2048,64]{1,2,0:T(8,128)(2,1)} %param.13) | copy-start | bytes 786436
  147.1 2.7 copy-start.1
  153.0 134.4 %all-gather.3.cloned.1.call-start = ((), (), s32[]{:S(2)}) async-start(), calls=%async_computation.3 | async-start | bytes 2621440 | tf_op jit(solution)/shard_map/all_gather | solution.py:55
  212.1 82.6 %copy-start.3 = (f32[768,64]{0,1:T(8,128)}, f32[768,64]{0,1:T(8,128)S(1)}, u32[]{:S(2)}) copy-start(f32[768,64]{0,1:T(8,128)S(1)} %fusion.15) | copy-start | bytes 589828
  228.9 12.5 %copy-start.5 = (s32[1,512]{1,0:T(1,128)S(1)}, s32[1,512]{1,0:T(1,128)}, u32[]{:S(2)}) copy-start(s32[1,512]{1,0:T(1,128)} %param.9) | copy-start | bytes 6148
  230.6 49.3 %all-to-all-start.1 = ((bf16[64,10,768]{2,1,0:T(8,128)(2,1)}), bf16[64,10,768]{2,1,0:T(8,128)(2,1)}, u32[]{:S(2)}, u32[]{:S(2)}) async-start(bf16[64,10,768]{2,1,0:T(8,128)(2,1)} %copy.33), calls=%async_computation.1 | async-start | bytes 3145728 | tf_op jit(solution)/shard_map/all_to_all | solution.py:31
  294.7 8.9 %copy-start.2 = (f32[2048,64]{0,1:T(8,128)S(1)}, f32[2048,64]{0,1:T(8,128)}, u32[]{:S(2)}) copy-start(f32[2048,64]{0,1:T(8,128)} %reduce_sum.32) | copy-start | bytes 1572868
Sparse Core Ops, SparseCore 0:
  153.1 44.1 all-reduce.1
  222.1 33.8 all-gather.2
